TPU v7x, 32 devices: a whole 2x2x4 slice. The times are simulated.
32 devices in a mesh: dp: 16 (over z, x, core), mp: 2 (over y).
Axes of the slice: x: 2, y: 2, z: 4, core: 2. Of those that a mesh axis runs over, the one named last changes fastest.
Arguments:
- frames_in: float32 [12288, 768], P(('dp', 'mp')), may hold values from -6 to 6
- frames_cot: float32 [12288, 768], P(('dp', 'mp')), may hold values from -6 to 6
- clip_ids: int32 [12288], replicated, may hold values from 0 to 16, never falling along the last dimension, each value on 1 to 768 neighbouring positions
- frame_mask: int32 [12288], replicated, may hold values 0 or 1
- norm_gain: float32 [2, 2, 768], replicated, may hold values from 0.25 to 1.75
- norm_bias: float32 [2, 2, 768], replicated, may hold values from -2 to 2
- qkv_weight: bfloat16 [2, 768, 3, 768], P(None, 'dp', None, 'mp'), as said below
- qv_bias: float32 [2, 2, 768], P(None, None, 'mp'), may hold values from -0.4 to 0.4
- proj_weight: bfloat16 [2, 768, 768], P(None, ('mp', 'dp')), may hold values from -4 to 4
- up_weight: bfloat16 [2, 768, 3072], P(None, 'dp', 'mp'), may hold values from -0.21875 to 0.21875
- up_bias: float32 [2, 3072], P(None, 'mp'), may hold values from -3 to 3
- down_weight: bfloat16 [2, 3072, 768], P(None, ('mp', 'dp')), may hold values from -0.109375 to 0.109375
- out_biases: float32 [2, 2, 768], replicated, may hold values from -2 to 2
Outputs:
- frames_out: float32 [12288, 768], P(('dp', 'mp'))
- frames_grad: float32 [12288, 768], P(('dp', 'mp'))
- grad_qkv: float32 [2, 768, 3, 768], P(None, 'dp', None, 'mp')
- grad_qv_bias: float32 [2, 2, 768], P(None, None, 'mp')
- grad_proj: float32 [2, 768, 768], P(None, ('mp', 'dp'))
- grad_up: float32 [2, 768, 3072], P(None, 'dp', 'mp')
- grad_up_bias: float32 [2, 3072], P(None, 'mp')
- grad_down: float32 [2, 3072, 768], P(None, ('mp', 'dp'))
- grad_gain: float32 [2, 2, 768], replicated
- grad_norm_bias: float32 [2, 2, 768], replicated
- grad_out_biases: float32 [2, 2, 768], replicated
Inputs may be any that keep to these rules, and one draw needn't show every extreme that they name: `clip_ids`: clip numbers never fall from one frame to the next; each clip holds 1 to 768 frames and one holds exactly 768. `qkv_weight`: projection weights for queries, keys and values.
All inputs are finite; a program needn't handle non-finite values.
Results may differ from a plain program's by a relative error of at most 0.013.
Values may be sent and summed in bfloat16 or wider, within the bound.
A program may use at most 320 MiB of HBM per device.

v0:
```python
import jax
import jax.numpy as jnp
from jax import lax
from jax.sharding import PartitionSpec as P

HD = 64
epsilon = 1e-05


def padded_2(block, sides, width):
    for axis, dim in sides:
        count = lax.axis_size(axis)
        forward = [(i, i + 1) for i in range(count - 1)]
        backward = [(target, source) for source, target in forward]
        low = lax.ppermute(
            lax.slice_in_dim(block, block.shape[dim] - width, None, axis=dim), axis, forward
        )
        high = lax.ppermute(lax.slice_in_dim(block, 0, width, axis=dim), axis, backward)
        block = jnp.concatenate([low, block, high], axis=dim)
    return block


def shifted(x, axis, by):
    size = lax.axis_size(axis)
    pairs = [(i, i + by) for i in range(size) if 0 <= i + by < size]
    return lax.ppermute(x, axis, pairs)


def norm_forward(values, gain_vec, bias_vec):
    row_mean = jnp.mean(values, axis=-1, keepdims=True)
    centred = values - row_mean
    inverse = lax.rsqrt(jnp.mean(centred * centred, axis=-1, keepdims=True) + epsilon)
    normed = centred * inverse
    return ((normed * gain_vec + bias_vec).astype(jnp.bfloat16), normed, inverse)


def norm_backward(grad_out, normed, inverse, gain_vec):
    scaled = grad_out * gain_vec
    projected = (
        scaled
        - jnp.mean(scaled, axis=-1, keepdims=True)
        - normed * jnp.mean(scaled * normed, axis=-1, keepdims=True)
    )
    return (inverse * projected, jnp.sum(grad_out * normed, axis=0), jnp.sum(grad_out, axis=0))


def gelu_value(preact):
    return 0.5 * preact * (1.0 + jax.scipy.special.erf(preact * 0.7071067811865476))


def gelu_slope(preact):
    return (
        0.5 * (1.0 + jax.scipy.special.erf(preact * 0.7071067811865476))
        + preact * jnp.exp(-0.5 * preact * preact) * 0.3989422804014327
    )


def padded(values, tok_span, fill):
    border = jnp.full((tok_span,) + values.shape[1:], fill, values.dtype)
    return jnp.concatenate([border, values, border], axis=0)


def block_mask(query_ids, block_start, key_ids, key_valid, tok_span):
    query_pos = block_start + jnp.arange(query_ids.shape[0], dtype=jnp.int32)
    key_pos = jnp.arange(key_ids.shape[0], dtype=jnp.int32)
    same_clip = query_ids[:, None] == key_ids[None, :]
    visible = (key_valid[None, :] == 1) | (key_pos[None, :] == query_pos[:, None] + tok_span)
    return same_clip & visible


def window_ids(clip_ids, frame_mask, tok_span):
    offset = lax.axis_index("dp") * tok_span
    ids_pad = padded(clip_ids, tok_span, -1)
    valid_pad = padded(frame_mask, tok_span, 0)
    return (
        lax.dynamic_slice_in_dim(ids_pad, offset + tok_span, tok_span, 0),
        lax.dynamic_slice_in_dim(ids_pad, offset, 3 * tok_span, 0),
        lax.dynamic_slice_in_dim(valid_pad, offset, 3 * tok_span, 0),
    )


def fetch_weights(qkv_weight, proj_weight, up_weight, down_weight, depth):
    return (
        lax.all_gather(qkv_weight[depth], "dp", axis=0, tiled=True),
        lax.all_gather(proj_weight[depth], "dp", axis=0, tiled=True),
        lax.all_gather(up_weight[depth], "dp", axis=0, tiled=True),
        lax.all_gather(down_weight[depth], "dp", axis=0, tiled=True),
    )


def gather_rows(values):
    return lax.all_gather(values, "mp", axis=0, tiled=True)


def sum_rows(left, right):
    return lax.psum_scatter(
        jnp.dot(left, right, preferred_element_type=jnp.float32),
        "mp",
        scatter_dimension=0,
        tiled=True,
    )


def block_scores(query, keys, query_ids, key_ids, key_valid, offset):
    tok_span = query.shape[0]
    allowed = block_mask(query_ids, offset, key_ids, key_valid, tok_span)
    scores = jnp.einsum("qhd,khd->hqk", query, keys, preferred_element_type=jnp.float32) * HD ** (
        -0.5
    )
    return (query, jnp.where(allowed[None], scores, -1e30))


def attend(query, key_vals, query_ids, key_ids, key_valid):
    tok_span = query.shape[0]
    n_blocks = (tok_span + 1023) // 1024
    block_rows = tok_span // n_blocks
    keys = key_vals[:, 0]
    values = key_vals[:, 1]

    def one_block(block_id):
        offset = block_id * block_rows
        query_block, scores = block_scores(query, keys, query_ids, key_ids, key_valid, offset)
        row_max = jnp.max(scores, axis=-1, keepdims=True)
        log_total = row_max + jnp.log(jnp.sum(jnp.exp(scores - row_max), axis=-1, keepdims=True))
        prob_low = jnp.exp(scores - log_total).astype(jnp.bfloat16)
        attended = jnp.einsum(
            "hqk,khd->qhd", prob_low, values, preferred_element_type=jnp.float32
        ).astype(jnp.bfloat16)
        return (attended, log_total[..., 0])

    attended, log_totals = lax.map(one_block, jnp.arange(n_blocks, dtype=jnp.int32))
    return (attended.reshape(query.shape), log_totals)


def attend_back(query, key_vals, attended, grad_attn, log_totals, query_ids, key_ids, key_valid):
    tok_span = query.shape[0]
    n_blocks = (tok_span + 1023) // 1024
    block_rows = tok_span // n_blocks
    score_scale = HD ** (-0.5)
    keys = key_vals[:, 0]
    values = key_vals[:, 1]

    def one_block(key_grads, block_id):
        offset = block_id * block_rows
        query_block, scores = block_scores(query, keys, query_ids, key_ids, key_valid, offset)
        prob_full = jnp.exp(scores - log_totals[block_id][..., None])
        prob_low = prob_full.astype(jnp.bfloat16)
        grad_prob = jnp.einsum(
            "qhd,khd->hqk", grad_attn, values, preferred_element_type=jnp.float32
        )
        delta_row = jnp.sum(grad_attn.astype(jnp.float32) * attended.astype(jnp.float32), axis=-1).T
        score_low = (prob_full * (grad_prob - delta_row[..., None])).astype(jnp.bfloat16)
        grad_query = (
            jnp.einsum("hqk,khd->qhd", score_low, keys, preferred_element_type=jnp.float32)
            * score_scale
        )
        grad_key = (
            jnp.einsum("hqk,qhd->khd", score_low, query_block, preferred_element_type=jnp.float32)
            * score_scale
        )
        grad_value = jnp.einsum(
            "hqk,qhd->khd", prob_low, grad_attn, preferred_element_type=jnp.float32
        )
        return (key_grads + jnp.stack([grad_key, grad_value], axis=1), grad_query)

    start = jnp.zeros((3 * tok_span, 2) + query.shape[1:], jnp.float32)
    key_grads, grad_query = lax.scan(one_block, start, jnp.arange(n_blocks, dtype=jnp.int32))
    return (grad_query.reshape(query.shape), key_grads)


def widen(piece, full_width, mp_index):
    out_shape = piece.shape[:-1] + (full_width,)
    return lax.dynamic_update_slice_in_dim(
        jnp.zeros(out_shape, jnp.float32), piece, mp_index * piece.shape[-1], piece.ndim - 1
    )


def layer_forward(
    state, matrices, gain_pair, bias_pair, qv_pair, up_vec, out_pair, query_ids, key_ids, key_valid
):
    qkv_mat, proj_mat, up_mat, down_mat = matrices
    head_cols = qkv_mat.shape[-1]
    first_norm, hat_one, inv_one = norm_forward(state, gain_pair[0], bias_pair[0])
    first_full = gather_rows(first_norm)
    tok_span = first_full.shape[0]
    bias_three = jnp.stack([qv_pair[0], jnp.zeros_like(qv_pair[0]), qv_pair[1]])
    qkv_proj = jnp.dot(
        first_full,
        qkv_mat.reshape(qkv_mat.shape[0], 3 * head_cols),
        preferred_element_type=jnp.float32,
    )
    qkv_proj = (qkv_proj.reshape(tok_span, 3, head_cols) + bias_three).astype(jnp.bfloat16)
    query = qkv_proj[:, 0].reshape(tok_span, head_cols // HD, HD)
    key_vals = qkv_proj[:, 1:].reshape(tok_span, 2 * head_cols)
    key_vals = padded_2(key_vals, (("dp", 0),), tok_span)
    key_vals = key_vals.reshape(3 * tok_span, 2, head_cols // HD, HD)
    attended, log_totals = attend(query, key_vals, query_ids, key_ids, key_valid)
    attn_flat = attended.reshape(tok_span, head_cols)
    middle = state + sum_rows(attn_flat, proj_mat) + out_pair[0]
    second_norm, hat_two, inv_two = norm_forward(middle, gain_pair[1], bias_pair[1])
    second_full = gather_rows(second_norm)
    preact = jnp.dot(second_full, up_mat, preferred_element_type=jnp.float32) + up_vec
    hidden = gelu_value(preact).astype(jnp.bfloat16)
    result = middle + sum_rows(hidden, down_mat) + out_pair[1]
    stored = {
        "hat_one": hat_one,
        "inv_one": inv_one,
        "first_full": first_full,
        "query": query,
        "key_vals": key_vals,
        "attended": attended,
        "log_totals": log_totals,
        "hat_two": hat_two,
        "inv_two": inv_two,
        "second_full": second_full,
        "preact": preact,
        "hidden": hidden,
    }
    return (stored, result)


def layer_backward(gradient, stored, matrices, gain_pair, query_ids, key_ids, key_valid):
    qkv_mat, proj_mat, up_mat, down_mat = matrices
    head_cols = qkv_mat.shape[-1]
    grad_full = gather_rows(gradient.astype(jnp.bfloat16))
    grad_down = jnp.dot(stored["hidden"].T, grad_full, preferred_element_type=jnp.float32)
    grad_pre = jnp.dot(grad_full, down_mat.T, preferred_element_type=jnp.float32) * gelu_slope(
        stored["preact"]
    )
    grad_upb = jnp.sum(grad_pre, axis=0)
    pre_low = grad_pre.astype(jnp.bfloat16)
    grad_up = jnp.dot(stored["second_full"].T, pre_low, preferred_element_type=jnp.float32)
    grad_second = sum_rows(pre_low, up_mat.T)
    back_two, gain_two, shift_two = norm_backward(
        grad_second, stored["hat_two"], stored["inv_two"], gain_pair[1]
    )
    grad_middle = gradient + back_two
    middle_full = gather_rows(grad_middle.astype(jnp.bfloat16))
    attended = stored["attended"]
    tok_span = attended.shape[0]
    grad_proj = jnp.dot(
        attended.reshape(tok_span, head_cols).T, middle_full, preferred_element_type=jnp.float32
    )
    grad_attn = jnp.dot(middle_full, proj_mat.T, preferred_element_type=jnp.float32).astype(
        jnp.bfloat16
    )
    grad_attn = grad_attn.reshape(attended.shape)
    grad_query, key_grads = attend_back(
        stored["query"],
        stored["key_vals"],
        attended,
        grad_attn,
        stored["log_totals"],
        query_ids,
        key_ids,
        key_valid,
    )
    key_grads = key_grads.reshape(3 * tok_span, 2 * head_cols)
    own_grads = key_grads[tok_span : 2 * tok_span]
    for step_by, piece in ((1, key_grads[2 * tok_span :]), (-1, key_grads[:tok_span])):
        own_grads = own_grads + shifted(piece.astype(jnp.bfloat16), "dp", step_by).astype(
            piece.dtype
        )
    grad_query = grad_query.reshape(tok_span, head_cols)
    grad_key = own_grads[:, :head_cols]
    grad_value = own_grads[:, head_cols:]
    grad_qv = jnp.stack([jnp.sum(grad_query, axis=0), jnp.sum(grad_value, axis=0)])
    qkv_low = (
        jnp.stack([grad_query, grad_key, grad_value], axis=1)
        .astype(jnp.bfloat16)
        .reshape(tok_span, 3 * head_cols)
    )
    grad_qkv = jnp.dot(stored["first_full"].T, qkv_low, preferred_element_type=jnp.float32).reshape(
        -1, 3, head_cols
    )
    grad_first = sum_rows(qkv_low, qkv_mat.reshape(-1, 3 * head_cols).T)
    back_one, gain_one, shift_one = norm_backward(
        grad_first, stored["hat_one"], stored["inv_one"], gain_pair[0]
    )
    new_grad = grad_middle + back_one
    mp_index = lax.axis_index("mp")
    mp_count = lax.axis_size("mp")
    small = (
        jnp.stack([gain_one, gain_two]),
        jnp.stack([shift_one, shift_two]),
        jnp.stack([jnp.sum(grad_middle, axis=0), jnp.sum(gradient, axis=0)]),
        widen(grad_qv, head_cols * mp_count, mp_index),
        widen(grad_upb, grad_upb.shape[0] * mp_count, mp_index),
    )
    return (new_grad, (grad_qkv, grad_proj, grad_up, grad_down), small)


def body(
    frames_in,
    frames_cot,
    clip_ids,
    frame_mask,
    norm_gain,
    norm_bias,
    qkv_weight,
    qv_bias,
    proj_weight,
    up_weight,
    up_bias,
    down_weight,
    out_biases,
):
    layers = qkv_weight.shape[0]
    tok_span = frames_in.shape[0] * lax.axis_size("mp")
    query_ids, key_ids, key_valid = window_ids(clip_ids, frame_mask, tok_span)
    stored_all = []
    state = frames_in
    for depth in range(layers):
        matrices = fetch_weights(qkv_weight, proj_weight, up_weight, down_weight, depth)
        stored, state = layer_forward(
            state,
            matrices,
            norm_gain[depth],
            norm_bias[depth],
            qv_bias[depth],
            up_bias[depth],
            out_biases[depth],
            query_ids,
            key_ids,
            key_valid,
        )
        stored_all.append(stored)
    gradient = frames_cot
    weight_grads = []
    small_grads = []
    for depth in range(layers - 1, -1, -1):
        matrices = fetch_weights(qkv_weight, proj_weight, up_weight, down_weight, depth)
        gradient, mats_grad, small = layer_backward(
            gradient, stored_all[depth], matrices, norm_gain[depth], query_ids, key_ids, key_valid
        )
        mats_grad = (
            lax.psum_scatter(mats_grad[0], "dp", scatter_dimension=0, tiled=True),
            lax.psum_scatter(mats_grad[1], "dp", scatter_dimension=0, tiled=True),
            lax.psum_scatter(mats_grad[2], "dp", scatter_dimension=0, tiled=True),
            lax.psum_scatter(mats_grad[3], "dp", scatter_dimension=0, tiled=True),
        )
        small = lax.psum((small[0], small[1], small[2], small[3], small[4]), ("dp", "mp"))
        weight_grads.insert(0, mats_grad)
        small_grads.insert(0, small)
    stacked_w = tuple((jnp.stack([entry[slot] for entry in weight_grads]) for slot in range(4)))
    stacked_s = tuple((jnp.stack([entry[slot] for entry in small_grads]) for slot in range(5)))
    mp_index = lax.axis_index("mp")
    head_cols = qv_bias.shape[-1]
    up_cols = up_bias.shape[-1]
    grad_qv = lax.dynamic_slice_in_dim(stacked_s[3], mp_index * head_cols, head_cols, 2)
    grad_upb = lax.dynamic_slice_in_dim(stacked_s[4], mp_index * up_cols, up_cols, 1)
    return (
        state,
        gradient,
        stacked_w[0],
        grad_qv,
        stacked_w[1],
        stacked_w[2],
        grad_upb,
        stacked_w[3],
        stacked_s[0],
        stacked_s[1],
        stacked_s[2],
    )


def solution(mesh):
    placed = (
        P(("dp", "mp"), None),
        P(("dp", "mp"), None),
        P(),
        P(),
        P(),
        P(),
        P(None, "dp", None, "mp"),
        P(None, None, "mp"),
        P(None, ("mp", "dp"), None),
        P(None, "dp", "mp"),
        P(None, "mp"),
        P(None, ("mp", "dp"), None),
        P(),
    )
    return jax.shard_map(
        body,
        mesh=mesh,
        in_specs=placed,
        out_specs=(
            P(("dp", "mp"), None),
            P(("dp", "mp"), None),
            P(None, "dp", None, "mp"),
            P(None, None, "mp"),
            P(None, ("mp", "dp"), None),
            P(None, "dp", "mp"),
            P(None, "mp"),
            P(None, ("mp", "dp"), None),
            P(),
            P(),
            P(),
        ),
        check_vma=False,
    )
```

profile of v0, /device:TPU:0, one launch (start us, length us, event | category | flops | bytes accessed | tf_op | source)
XLA Modules:
  0.0 1947.3 jit_solution(16931985044161411071)
XLA Ops:
  14.8 39.2 %all-gather.39.cloned.1.call-done = bf16[1,768,3,384]{3,1,2,0:T(8,128)(2,1)} async-done(((bf16[1,48,3,384]{3,1,2,0:T(8,128)(2,1)}), bf16[1,768,3,384]{3,1,2,0:T(8,128)(2,1)}) %all-gather.39.cloned.1.call-update) | async-done | bytes 1769488 | tf_op jit(solution)/shard_map/all_gather | solution.py:84
  88.5 39.6 %all-gather.1 = bf16[1,384,768]{2,1,0:T(8,128)(2,1)} all-gather(bf16[1,24,768]{2,1,0:T(8,128)(2,1)S(1)} %get-tuple-element.207), channel_id=3, replica_groups=mesh['dp'=16,'mp'=2] {'dp'}, dimensions={1}, use_global_device_ids=true | all-gather | bytes 626688 | tf_op jit(solution)/shard_map/all_gather | solution.py:85
  198.3 32.1 %reduce-scatter.17.cloned.1.call-done = f32[384,768]{1,0:T(8,128)} async-done(((f32[768,768]{1,0:T(8,128)}), f32[384,768]{1,0:T(8,128)}) %reduce-scatter.17.cloned.1.call-update) | async-done | bytes 1179664 | tf_op jit(solution)/shard_map/reduce_scatter | solution.py:96
  235.6 39.8 %all-gather.41.cloned.1.call-done = bf16[1,768,1536]{2,1,0:T(8,128)(2,1)} async-done(((bf16[1,48,1536]{2,1,0:T(8,128)(2,1)}), bf16[1,768,1536]{2,1,0:T(8,128)(2,1)}) %all-gather.41.cloned.1.call-update) | async-done | bytes 2359312 | tf_op jit(solution)/shard_map/all_gather | solution.py:86
  305.9 38.0 %all-gather.43.cloned.1.call-done = bf16[1,1536,768]{2,1,0:T(8,128)(2,1)} async-done(((bf16[1,96,768]{2,1,0:T(8,128)(2,1)}), bf16[1,1536,768]{2,1,0:T(8,128)(2,1)}) %all-gather.43.cloned.1.call-update) | async-done | bytes 2359312 | tf_op jit(solution)/shard_map/all_gather | solution.py:87
  350.5 32.9 %reduce-scatter.19.cloned.1.call-done = f32[384,768]{1,0:T(8,128)} async-done(((f32[768,768]{1,0:T(8,128)}), f32[384,768]{1,0:T(8,128)}) %reduce-scatter.19.cloned.1.call-update) | async-done | bytes 1179664 | tf_op jit(solution)/shard_map/reduce_scatter | solution.py:96
  387.1 39.1 %all-gather.45.cloned.1.call-done = bf16[1,768,3,384]{3,1,2,0:T(8,128)(2,1)} async-done(((bf16[1,48,3,384]{3,1,2,0:T(8,128)(2,1)}), bf16[1,768,3,384]{3,1,2,0:T(8,128)(2,1)}) %all-gather.45.cloned.1.call-update) | async-done | bytes 1769488 | tf_op jit(solution)/shard_map/all_gather | solution.py:84
  457.2 39.2 %all-gather.5 = bf16[1,384,768]{2,1,0:T(8,128)(2,1)S(1)} all-gather(bf16[1,24,768]{2,1,0:T(8,128)(2,1)S(1)} %copy-done.50), channel_id=7, replica_groups=mesh['dp'=16,'mp'=2] {'dp'}, dimensions={1}, use_global_device_ids=true | all-gather | bytes 626688 | tf_op jit(solution)/shard_map/all_gather | solution.py:85
  557.9 33.6 %reduce-scatter.21.cloned.1.call-done = f32[384,768]{1,0:T(8,128)} async-done(((f32[768,768]{1,0:T(8,128)}), f32[384,768]{1,0:T(8,128)}) %reduce-scatter.21.cloned.1.call-update) | async-done | bytes 1179664 | tf_op jit(solution)/shard_map/reduce_scatter | solution.py:96
  599.2 37.5 %all-gather.47.cloned.1.call-done = bf16[1,768,1536]{2,1,0:T(8,128)(2,1)} async-done(((bf16[1,48,1536]{2,1,0:T(8,128)(2,1)}), bf16[1,768,1536]{2,1,0:T(8,128)(2,1)}) %all-gather.47.cloned.1.call-update) | async-done | bytes 2359312 | tf_op jit(solution)/shard_map/all_gather | solution.py:86
  685.1 44.5 %all-gather.49.cloned.1.call-done = bf16[1,1536,768]{2,1,0:T(8,128)(2,1)} async-done(((bf16[1,96,768]{2,1,0:T(8,128)(2,1)}), bf16[1,1536,768]{2,1,0:T(8,128)(2,1)}) %all-gather.49.cloned.1.call-update) | async-done | bytes 2359312 | tf_op jit(solution)/shard_map/all_gather | solution.py:87
  777.9 33.6 %reduce-scatter.23.cloned.1.call-done = f32[384,768]{1,0:T(8,128)} async-done(((f32[768,768]{1,0:T(8,128)}), f32[384,768]{1,0:T(8,128)}) %reduce-scatter.23.cloned.1.call-update) | async-done | bytes 1179664 | tf_op jit(solution)/shard_map/reduce_scatter | solution.py:96
  941.3 41.2 %reduce-scatter.27.cloned.1.call-done = f32[384,768]{1,0:T(8,128)} async-done(((f32[768,768]{1,0:T(8,128)}), f32[384,768]{1,0:T(8,128)}) %reduce-scatter.27.cloned.1.call-update) | async-done | bytes 1179664 | tf_op jit(solution)/shard_map/reduce_scatter | solution.py:96
  1022.2 34.9 %reduce-scatter.29.cloned.1.call-done = f32[384,768]{1,0:T(8,128)} async-done(((f32[768,768]{1,0:T(8,128)}), f32[384,768]{1,0:T(8,128)}) %reduce-scatter.29.cloned.1.call-update) | async-done | bytes 1179664 | tf_op jit(solution)/shard_map/reduce_scatter | solution.py:96
  1107.1 28.2 %multiply_convert_fusion = bf16[6,768,2304]{2,1,0:T(8,128)(2,1)} fusion(f32[6,768,2304]{2,1,0:T(8,128)} %get-tuple-element.215, bf16[768,6,64]{0,2,1:T(8,128)(2,1)S(1)} %bitcast.280, f32[6,768]{1,0:T(8,128)S(1)} %bitcast.292, f32[6,768]{1,0:T(8,128)S(1)} %copy-done.73, pred[768,2304]{1,0:T(8,128)(4,1)S(1)} %fusion.7, ...), kind=kOutput, calls=%fused_computation | convolution fusion | flops 1422655488 | bytes 67866624 | tf_op jit(solution)/shard_map/while/body/eval_jaxpr/qhd,khd->hqk/dot_general | solution.py:148
  1260.2 42.7 %reduce-scatter.47.cloned.1.call-done = f32[96,768]{1,0:T(8,128)} async-done(((f32[1536,768]{1,0:T(8,128)}), f32[96,768]{1,0:T(8,128)}) %reduce-scatter.47.cloned.1.call-update) | async-done | bytes 294928 | tf_op jit(solution)/shard_map/reduce_scatter | solution.py:340
  1302.9 78.5 %reduce-scatter.45.cloned.1.call-done = f32[96,768]{1,0:T(8,128)} async-done(((f32[1536,768]{1,0:T(8,128)}), f32[96,768]{1,0:T(8,128)}) %reduce-scatter.45.cloned.1.call-update) | async-done | bytes 294928 | tf_op jit(solution)/shard_map/reduce_scatter | solution.py:340
  1383.3 76.8 %reduce-scatter.43.cloned.1.call-done = f32[48,1536]{1,0:T(8,128)} async-done(((f32[768,1536]{1,0:T(8,128)}), f32[48,1536]{1,0:T(8,128)}) %reduce-scatter.43.cloned.1.call-update) | async-done | bytes 294928 | tf_op jit(solution)/shard_map/reduce_scatter | solution.py:339
  1460.1 78.5 %reduce-scatter.41.cloned.1.call-done = f32[48,1536]{1,0:T(8,128)} async-done(((f32[768,1536]{1,0:T(8,128)}), f32[48,1536]{1,0:T(8,128)}) %reduce-scatter.41.cloned.1.call-update) | async-done | bytes 294928 | tf_op jit(solution)/shard_map/reduce_scatter | solution.py:339
  1540.5 59.0 %reduce-scatter.39.cloned.1.call-done = f32[24,768]{1,0:T(8,128)} async-done(((f32[384,768]{1,0:T(8,128)}), f32[24,768]{1,0:T(8,128)}) %reduce-scatter.39.cloned.1.call-update) | async-done | bytes 73744 | tf_op jit(solution)/shard_map/reduce_scatter | solution.py:338
  1599.5 60.9 %reduce-scatter.37.cloned.1.call-done = f32[24,768]{1,0:T(8,128)} async-done(((f32[384,768]{1,0:T(8,128)}), f32[24,768]{1,0:T(8,128)}) %reduce-scatter.37.cloned.1.call-update) | async-done | bytes 73744 | tf_op jit(solution)/shard_map/reduce_scatter | solution.py:338
  1664.7 128.0 %all-reduce.3.cloned.1.call-done = (f32[1,2,768]{2,1,0:T(2,128)}, f32[1,2,768]{2,1,0:T(2,128)}, f32[1,3072]{1,0:T(1,128)}, f32[1,3072]{1,0:T(1,128)}, f32[1,2,76...) async-done(((f32[1,2,768]{2,1,0:T(2,128)}, f32[1,2,768]{2,1,0:T(2,128)}, ...) | async-done | bytes 73744 | tf_op jit(solution)/shard_map/psum | solution.py:342
  1799.2 68.4 %reduce-scatter.35.cloned.1.call-done = f32[48,3,384]{2,0,1:T(8,128)} async-done(((f32[768,3,384]{2,0,1:T(8,128)}), f32[48,3,384]{2,0,1:T(8,128)}) %reduce-scatter.35.cloned.1.call-update) | async-done | bytes 221200 | tf_op jit(solution)/shard_map/reduce_scatter | solution.py:337
  1867.6 70.9 %reduce-scatter.33.cloned.1.call-done = f32[48,3,384]{2,0,1:T(8,128)} async-done(((f32[768,3,384]{2,0,1:T(8,128)}), f32[48,3,384]{2,0,1:T(8,128)}) %reduce-scatter.33.cloned.1.call-update) | async-done | bytes 221200 | tf_op jit(solution)/shard_map/reduce_scatter | solution.py:337
  (452 shorter events, 714.8 us)
Async XLA Ops:
  13.4 217.0 %reduce-scatter.17.cloned.1.call-start = ((), (), s32[]{:S(2)}) async-start(), calls=%async_computation.17 | async-start | bytes 3538944 | tf_op jit(solution)/shard_map/reduce_scatter | solution.py:96
  195.9 79.5 %all-gather.41.cloned.1.call-start = ((), (), s32[]{:S(2)}) async-start(), calls=%async_computation.41 | async-start | bytes 2506752 | tf_op jit(solution)/shard_map/all_gather | solution.py:86
  197.6 101.3 %all-gather.25.cloned.1.call-start = ((), (), s32[]{:S(2)}) async-start(), calls=%async_computation.18 | async-start | bytes 1769472 | tf_op jit(solution)/shard_map/all_gather | solution.py:92
  234.0 110.0 %all-gather.43.cloned.1.call-start = ((), (), s32[]{:S(2)}) async-start(), calls=%async_computation.42 | async-start | bytes 2506752 | tf_op jit(solution)/shard_map/all_gather | solution.py:87
  234.8 148.6 %reduce-scatter.19.cloned.1.call-start = ((), (), s32[]{:S(2)}) async-start(), calls=%async_computation.19 | async-start | bytes 3538944 | tf_op jit(solution)/shard_map/reduce_scatter | solution.py:96
  350.5 99.3 %all-gather.27.cloned.1.call-start = ((), (), s32[]{:S(2)}) async-start(), calls=%async_computation.20 | async-start | bytes 1769472 | tf_op jit(solution)/shard_map/all_gather | solution.py:92
  387.0 204.5 %reduce-scatter.21.cloned.1.call-start = ((), (), s32[]{:S(2)}) async-start(), calls=%async_computation.21 | async-start | bytes 3538944 | tf_op jit(solution)/shard_map/reduce_scatter | solution.py:96
  557.1 79.6 %all-gather.47.cloned.1.call-start = ((), (), s32[]{:S(2)}) async-start(), calls=%async_computation.44 | async-start | bytes 2506752 | tf_op jit(solution)/shard_map/all_gather | solution.py:86
  557.8 102.4 %all-gather.29.cloned.1.call-start = ((), (), s32[]{:S(2)}) async-start(), calls=%async_computation.22 | async-start | bytes 1769472 | tf_op jit(solution)/shard_map/all_gather | solution.py:92
  595.1 90.0 %all-gather.31.cloned.1.call-start = ((), (), s32[]{:S(2)}) async-start(), calls=%async_computation.24 | async-start | bytes 1769472 | tf_op jit(solution)/shard_map/all_gather | solution.py:92
  598.4 131.2 %all-gather.49.cloned.1.call-start = ((), (), s32[]{:S(2)}) async-start(), calls=%async_computation.45 | async-start | bytes 2506752 | tf_op jit(solution)/shard_map/all_gather | solution.py:87
  598.9 175.6 %reduce-scatter.25.cloned.1.call-start = ((), (), s32[]{:S(2)}) async-start(), calls=%async_computation.25 | async-start | bytes 3538944 | tf_op jit(solution)/shard_map/reduce_scatter | solution.py:96
  746.7 94.0 %all-gather.33.cloned.1.call-start = ((), (), s32[]{:S(2)}) async-start(), calls=%async_computation.26 | async-start | bytes 1769472 | tf_op jit(solution)/shard_map/all_gather | solution.py:92
  817.8 164.6 %reduce-scatter.27.cloned.1.call-start = ((), (), s32[]{:S(2)}) async-start(), calls=%async_computation.27 | async-start | bytes 3538944 | tf_op jit(solution)/shard_map/reduce_scatter | solution.py:96
  1062.7 179.0 %reduce-scatter.31.cloned.1.call-start = ((), (), s32[]{:S(2)}) async-start(), calls=%async_computation.31 | async-start | bytes 3538944 | tf_op jit(solution)/shard_map/reduce_scatter | solution.py:96
  1182.4 120.5 %reduce-scatter.47.cloned.1.call-start = ((), (), s32[]{:S(2)}) async-start(), calls=%async_computation.39 | async-start | bytes 5013504 | tf_op jit(solution)/shard_map/reduce_scatter | solution.py:340
  1189.5 191.9 %reduce-scatter.45.cloned.1.call-start = ((), (), s32[]{:S(2)}) async-start(), calls=%async_computation.38 | async-start | bytes 5013504 | tf_op jit(solution)/shard_map/reduce_scatter | solution.py:340
  1196.7 263.4 %reduce-scatter.43.cloned.1.call-start = ((), (), s32[]{:S(2)}) async-start(), calls=%async_computation.37 | async-start | bytes 5013504 | tf_op jit(solution)/shard_map/reduce_scatter | solution.py:339
  1203.9 334.7 %reduce-scatter.41.cloned.1.call-start = ((), (), s32[]{:S(2)}) async-start(), calls=%async_computation.36 | async-start | bytes 5013504 | tf_op jit(solution)/shard_map/reduce_scatter | solution.py:339
  1211.0 388.5 %reduce-scatter.39.cloned.1.call-start = ((), (), s32[]{:S(2)}) async-start(), calls=%async_computation.35 | async-start | bytes 1253376 | tf_op jit(solution)/shard_map/reduce_scatter | solution.py:338
  1214.1 446.2 %reduce-scatter.37.cloned.1.call-start = ((), (), s32[]{:S(2)}) async-start(), calls=%async_computation.34 | async-start | bytes 1253376 | tf_op jit(solution)/shard_map/reduce_scatter | solution.py:338
  1217.8 574.8 %all-reduce.3.cloned.1.call-start = ((), (), s32[]{:S(2)}) async-start(), calls=%async_computation.46 | async-start | bytes 147456 | tf_op jit(solution)/shard_map/psum | solution.py:342
  1246.0 621.6 %reduce-scatter.35.cloned.1.call-start = ((), (), s32[]{:S(2)}) async-start(), calls=%async_computation.33 | async-start | bytes 3760128 | tf_op jit(solution)/shard_map/reduce_scatter | solution.py:337
  1251.0 687.5 %reduce-scatter.33.cloned.1.call-start = ((), (), s32[]{:S(2)}) async-start(), calls=%async_computation.32 | async-start | bytes 3760128 | tf_op jit(solution)/shard_map/reduce_scatter | solution.py:337
  (112 other events, 3638.4 us)
Sparse Core Ops, SparseCore 0:
  10.9 43.1 all-gather.38
  196.0 34.2 reduce-scatter.16
  233.1 42.2 all-gather.40
  301.6 42.2 all-gather.42
  349.9 33.5 reduce-scatter.18
  385.7 40.4 all-gather.44
  557.2 34.2 reduce-scatter.20
  594.4 42.2 all-gather.46
  687.2 42.2 all-gather.48
  741.0 33.5 reduce-scatter.24
  776.6 34.7 reduce-scatter.22
  817.9 22.7 all-gather.32
  941.4 41.0 reduce-scatter.26
  1022.3 34.7 reduce-scatter.28
  1182.5 40.8 reduce-scatter.30
  1227.3 75.5 reduce-scatter.46
  1306.6 74.7 reduce-scatter.44
  1385.3 74.7 reduce-scatter.42
  1463.8 74.7 reduce-scatter.40
  1542.1 57.3 reduce-scatter.38
  1603.1 57.1 reduce-scatter.36
  1667.9 124.6 all-reduce.2
  1796.3 71.2 reduce-scatter.34
  1871.5 66.9 reduce-scatter.32
  (7 shorter events, 153.7 us)
where the time goes:
time: 1950 us
  waiting for transfers between devices  1310 us (67%)
  matrix products  312 us (16%)
  other arithmetic  129 us (7%)
  blocking collectives  78.8 us (4%)
  local copies, waits for them, and re-layouts  73.5 us (4%)
  starting transfers between devices  23.5 us (1%)
    reduce_scatter x8, waiting for transfers between devices, sum_rows(): lax.psum_scatter(jnp.dot(left, right, preferred_element_type=jnp.float32)...  236 us
    all_gather x8, waiting for transfers between devices, gather_rows(): return lax.all_gather(values, 'mp', axis=0, tiled=True)  175 us
    reduce_scatter x2, waiting for transfers between devices, body(): lax.psum_scatter(mats_grad[2], 'dp', scatter_dimension=0, tiled=True)  155 us
    reduce_scatter x2, waiting for transfers between devices, body(): lax.psum_scatter(mats_grad[0], 'dp', scatter_dimension=0, tiled=True)  139 us
    psum x1, waiting for transfers between devices, body(): lax.psum((small[0], small[1], small[2], small[3], small[4]), ('dp', 'mp'))  128 us
    reduce_scatter x2, waiting for transfers between devices, body(): lax.psum_scatter(mats_grad[3], 'dp', scatter_dimension=0, tiled=True)  121 us
    reduce_scatter x2, waiting for transfers between devices, body(): lax.psum_scatter(mats_grad[1], 'dp', scatter_dimension=0, tiled=True)  120 us
    all_gather x2, waiting for transfers between devices, fetch_weights(): lax.all_gather(down_weight[depth], 'dp', axis=0, tiled=True)  82.5 us
  transfers between devices with their start and end apart: 39, of which 30 were waited for; matrix products, arithmetic and copies ran while one was open for 9% of the time, Pallas kernels for 0%

commit v1 on v0

--- a/solution.py
+++ b/solution.py
@@ -5,6 +5,18 @@
 
 HD = 64
 epsilon = 1e-05
+
+
+def gather_by_bits(array, axis, dim):
+    ways, here, step = (lax.axis_size(axis), lax.axis_index(axis), array.shape[dim])
+    line, have = (array, 1)
+    while have < ways:
+        line = jnp.concatenate(
+            [line, lax.ppermute(line, axis, [(d, (d - have) % ways) for d in range(ways)])],
+            axis=dim,
+        )
+        have = 2 * have
+    return jnp.roll(line, here * step, axis=dim)
 
 
 def padded_2(block, sides, width):
@@ -89,7 +101,7 @@
 
 
 def gather_rows(values):
-    return lax.all_gather(values, "mp", axis=0, tiled=True)
+    return gather_by_bits(values, "mp", 0)
 
 
 def sum_rows(left, right):

time: 1950 us -> 1840 us (0.944)
  waiting for transfers between devices: 1310 us -> 1170 us
  other arithmetic: 129 us -> 149 us
    all_gather x8 -> x0, waiting for transfers between devices: 175 us -> none  [gather_rows(): return lax.all_gather(values, 'mp', axis=0, tiled=True)]
    ppermute x0 -> x8, waiting for transfers between devices: none -> 84.3 us  [gather_by_bits(): lax.ppermute(line, axis, [(d, (d - have) % ways) for d in range(ways)])]
    reduce_scatter x2, waiting for transfers between devices: 121 us -> 155 us  [body(): lax.psum_scatter(mats_grad[3], 'dp', scatter_dimension=0, tiled=True)]
    reduce_scatter x2, waiting for transfers between devices: 120 us -> 85.7 us  [body(): lax.psum_scatter(mats_grad[1], 'dp', scatter_dimension=0, tiled=True)]
    all_gather x2, waiting for transfers between devices: 77.2 us -> 43.3 us  [fetch_weights(): lax.all_gather(up_weight[depth], 'dp', axis=0, tiled=True)]
    concatenate x0 -> x5, other arithmetic: none -> 20.5 us  [gather_by_bits(): return jnp.roll(line, here * step, axis=dim)]
  transfers between devices with their start and end apart: 39 -> 39, of which waited for: 30 -> 28; matrix products, arithmetic and copies ran while one was open for 9% -> 10% of each run, Pallas kernels for 0% -> 0%
where the time goes in v1:
time: 1840 us; the launch traced here: 1830 us
  waiting for transfers between devices  1170 us (64%)
  matrix products  303 us (16%)
  other arithmetic  149 us (8%)
  local copies, waits for them, and re-layouts  87.4 us (5%)
  blocking collectives  79.2 us (4%)
  starting transfers between devices  29.5 us (2%)
    reduce_scatter x8, waiting for transfers between devices, sum_rows(): lax.psum_scatter(jnp.dot(left, right, preferred_element_type=jnp.float32)...  239 us
    reduce_scatter x2, waiting for transfers between devices, body(): lax.psum_scatter(mats_grad[3], 'dp', scatter_dimension=0, tiled=True)  155 us
    reduce_scatter x2, waiting for transfers between devices, body(): lax.psum_scatter(mats_grad[2], 'dp', scatter_dimension=0, tiled=True)  155 us
    reduce_scatter x2, waiting for transfers between devices, body(): lax.psum_scatter(mats_grad[0], 'dp', scatter_dimension=0, tiled=True)  139 us
    psum x1, waiting for transfers between devices, body(): lax.psum((small[0], small[1], small[2], small[3], small[4]), ('dp', 'mp'))  129 us
    reduce_scatter x2, waiting for transfers between devices, body(): lax.psum_scatter(mats_grad[1], 'dp', scatter_dimension=0, tiled=True)  85.7 us
    ppermute x8, waiting for transfers between devices, gather_by_bits(): lax.ppermute(line, axis, [(d, (d - have) % ways) for d in range(ways)])  84.3 us
    all_gather x2, blocking collectives, fetch_weights(): lax.all_gather(proj_weight[depth], 'dp', axis=0, tiled=True)  79.2 us
  transfers between devices with their start and end apart: 39, of which 28 were waited for; matrix products, arithmetic and copies ran while one was open for 10% of the time, Pallas kernels for 0%

profile of v1, /device:TPU:0, one launch (start us, length us, event | category | flops | bytes accessed | tf_op | source)
XLA Modules:
  0.0 1830.3 jit_solution(3002592605052659240)
XLA Ops:
  67.4 39.1 %all-gather.1 = bf16[1,384,768]{2,1,0:T(8,128)(2,1)} all-gather(bf16[1,24,768]{2,1,0:T(8,128)(2,1)S(1)} %get-tuple-element.208), channel_id=3, replica_groups=mesh['dp'=16,'mp'=2] {'dp'}, dimensions={1}, use_global_device_ids=true | all-gather | bytes 626688 | tf_op jit(solution)/shard_map/all_gather | solution.py:97
  179.6 29.7 %reduce-scatter.17.cloned.1.call-done = f32[384,768]{1,0:T(8,128)} async-done(((f32[768,768]{1,0:T(8,128)}), f32[384,768]{1,0:T(8,128)}) %reduce-scatter.17.cloned.1.call-update) | async-done | bytes 1179664 | tf_op jit(solution)/shard_map/reduce_scatter | solution.py:108
  230.3 23.9 %all-gather.17.cloned.1.call-done = bf16[1,768,1536]{2,1,0:T(8,128)(2,1)} async-done(((bf16[1,48,1536]{2,1,0:T(8,128)(2,1)}), bf16[1,768,1536]{2,1,0:T(8,128)(2,1)}) %all-gather.17.cloned.1.call-update) | async-done | bytes 2359312 | tf_op jit(solution)/shard_map/all_gather | solution.py:98
  260.0 38.0 %all-gather.19.cloned.1.call-done = bf16[1,1536,768]{2,1,0:T(8,128)(2,1)} async-done(((bf16[1,96,768]{2,1,0:T(8,128)(2,1)}), bf16[1,1536,768]{2,1,0:T(8,128)(2,1)}) %all-gather.19.cloned.1.call-update) | async-done | bytes 2359312 | tf_op jit(solution)/shard_map/all_gather | solution.py:99
  304.7 32.8 %reduce-scatter.19.cloned.1.call-done = f32[384,768]{1,0:T(8,128)} async-done(((f32[768,768]{1,0:T(8,128)}), f32[384,768]{1,0:T(8,128)}) %reduce-scatter.19.cloned.1.call-update) | async-done | bytes 1179664 | tf_op jit(solution)/shard_map/reduce_scatter | solution.py:108
  340.7 39.9 %all-gather.21.cloned.1.call-done = bf16[1,768,3,384]{3,1,2,0:T(8,128)(2,1)} async-done(((bf16[1,48,3,384]{3,1,2,0:T(8,128)(2,1)}), bf16[1,768,3,384]{3,1,2,0:T(8,128)(2,1)}) %all-gather.21.cloned.1.call-update) | async-done | bytes 1769488 | tf_op jit(solution)/shard_map/all_gather | solution.py:96
  393.9 40.1 %all-gather.5 = bf16[1,384,768]{2,1,0:T(8,128)(2,1)} all-gather(bf16[1,24,768]{2,1,0:T(8,128)(2,1)S(1)} %copy-done.65), channel_id=7, replica_groups=mesh['dp'=16,'mp'=2] {'dp'}, dimensions={1}, use_global_device_ids=true | all-gather | bytes 626688 | tf_op jit(solution)/shard_map/all_gather | solution.py:97
  501.4 40.8 %reduce-scatter.21.cloned.1.call-done = f32[384,768]{1,0:T(8,128)} async-done(((f32[768,768]{1,0:T(8,128)}), f32[384,768]{1,0:T(8,128)}) %reduce-scatter.21.cloned.1.call-update) | async-done | bytes 1179664 | tf_op jit(solution)/shard_map/reduce_scatter | solution.py:108
  594.0 36.5 %all-gather.25.cloned.1.call-done = bf16[1,1536,768]{2,1,0:T(8,128)(2,1)} async-done(((bf16[1,96,768]{2,1,0:T(8,128)(2,1)}), bf16[1,1536,768]{2,1,0:T(8,128)(2,1)}) %all-gather.25.cloned.1.call-update) | async-done | bytes 2359312 | tf_op jit(solution)/shard_map/all_gather | solution.py:99
  647.9 27.6 %reduce-scatter.25.cloned.1.call-done = f32[384,768]{1,0:T(8,128)} async-done(((f32[768,768]{1,0:T(8,128)}), f32[384,768]{1,0:T(8,128)}) %reduce-scatter.25.cloned.1.call-update) | async-done | bytes 1179664 | tf_op jit(solution)/shard_map/reduce_scatter | solution.py:108
  679.4 33.1 %reduce-scatter.23.cloned.1.call-done = f32[384,768]{1,0:T(8,128)} async-done(((f32[768,768]{1,0:T(8,128)}), f32[384,768]{1,0:T(8,128)}) %reduce-scatter.23.cloned.1.call-update) | async-done | bytes 1179664 | tf_op jit(solution)/shard_map/reduce_scatter | solution.py:108
  756.0 28.1 %multiply_convert_fusion.1 = bf16[6,768,2304]{2,1,0:T(8,128)(2,1)} fusion(f32[6,768,2304]{2,1,0:T(8,128)} %get-tuple-element.220, bf16[768,6,64]{0,2,1:T(8,128)(2,1)S(1)} %bitcast.281, f32[6,768]{1,0:T(8,128)S(1)} %bitcast.291, f32[6,768]{1,0:T(8,128)S(1)} %copy-done.89, pred[768,2304]{1,0:T(8,128)(4,1)S(1)} %fusion.7, ...), kind=kOutput, calls=%fused_computation.1 | convolution fusion | flops 1422655488 | bytes 67866624 | tf_op jit(solution)/shard_map/while/body/eval_jaxpr/qhd,khd->hqk/dot_general | solution.py:160
  835.6 39.7 %reduce-scatter.27.cloned.1.call-done = f32[384,768]{1,0:T(8,128)} async-done(((f32[768,768]{1,0:T(8,128)}), f32[384,768]{1,0:T(8,128)}) %reduce-scatter.27.cloned.1.call-update) | async-done | bytes 1179664 | tf_op jit(solution)/shard_map/reduce_scatter | solution.py:108
  909.5 34.9 %reduce-scatter.29.cloned.1.call-done = f32[384,768]{1,0:T(8,128)} async-done(((f32[768,768]{1,0:T(8,128)}), f32[384,768]{1,0:T(8,128)}) %reduce-scatter.29.cloned.1.call-update) | async-done | bytes 1179664 | tf_op jit(solution)/shard_map/reduce_scatter | solution.py:108
  988.9 28.1 %multiply_convert_fusion = bf16[6,768,2304]{2,1,0:T(8,128)(2,1)} fusion(f32[6,768,2304]{2,1,0:T(8,128)} %get-tuple-element.216, bf16[768,6,64]{0,2,1:T(8,128)(2,1)S(1)} %bitcast.278, f32[6,768]{1,0:T(8,128)S(1)} %bitcast.290, f32[6,768]{1,0:T(8,128)S(1)} %copy-done.88, pred[768,2304]{1,0:T(8,128)(4,1)S(1)} %fusion.7, ...), kind=kOutput, calls=%fused_computation | convolution fusion | flops 1422655488 | bytes 67866624 | tf_op jit(solution)/shard_map/while/body/eval_jaxpr/qhd,khd->hqk/dot_general | solution.py:160
  1143.2 25.0 %reduce-scatter.39.cloned.1.call-done = f32[24,768]{1,0:T(8,128)} async-done(((f32[384,768]{1,0:T(8,128)}), f32[24,768]{1,0:T(8,128)}) %reduce-scatter.39.cloned.1.call-update) | async-done | bytes 73744 | tf_op jit(solution)/shard_map/reduce_scatter | solution.py:350
  1168.1 60.8 %reduce-scatter.37.cloned.1.call-done = f32[24,768]{1,0:T(8,128)} async-done(((f32[384,768]{1,0:T(8,128)}), f32[24,768]{1,0:T(8,128)}) %reduce-scatter.37.cloned.1.call-update) | async-done | bytes 73744 | tf_op jit(solution)/shard_map/reduce_scatter | solution.py:350
  1230.5 76.8 %reduce-scatter.47.cloned.1.call-done = f32[96,768]{1,0:T(8,128)} async-done(((f32[1536,768]{1,0:T(8,128)}), f32[96,768]{1,0:T(8,128)}) %reduce-scatter.47.cloned.1.call-update) | async-done | bytes 294928 | tf_op jit(solution)/shard_map/reduce_scatter | solution.py:352
  1307.3 78.5 %reduce-scatter.45.cloned.1.call-done = f32[96,768]{1,0:T(8,128)} async-done(((f32[1536,768]{1,0:T(8,128)}), f32[96,768]{1,0:T(8,128)}) %reduce-scatter.45.cloned.1.call-update) | async-done | bytes 294928 | tf_op jit(solution)/shard_map/reduce_scatter | solution.py:352
  1387.7 76.7 %reduce-scatter.43.cloned.1.call-done = f32[48,1536]{1,0:T(8,128)} async-done(((f32[768,1536]{1,0:T(8,128)}), f32[48,1536]{1,0:T(8,128)}) %reduce-scatter.43.cloned.1.call-update) | async-done | bytes 294928 | tf_op jit(solution)/shard_map/reduce_scatter | solution.py:351
  1464.5 78.5 %reduce-scatter.41.cloned.1.call-done = f32[48,1536]{1,0:T(8,128)} async-done(((f32[768,1536]{1,0:T(8,128)}), f32[48,1536]{1,0:T(8,128)}) %reduce-scatter.41.cloned.1.call-update) | async-done | bytes 294928 | tf_op jit(solution)/shard_map/reduce_scatter | solution.py:351
  1547.0 128.6 %all-reduce.3.cloned.1.call-done = (f32[1,2,768]{2,1,0:T(2,128)}, f32[1,2,768]{2,1,0:T(2,128)}, f32[1,3072]{1,0:T(1,128)}, f32[1,3072]{1,0:T(1,128)}, f32[1,2,76...) async-done(((f32[1,2,768]{2,1,0:T(2,128)}, f32[1,2,768]{2,1,0:T(2,128)}, ...) | async-done | bytes 73744 | tf_op jit(solution)/shard_map/psum | solution.py:354
  1682.2 68.5 %reduce-scatter.35.cloned.1.call-done = f32[48,3,384]{2,0,1:T(8,128)} async-done(((f32[768,3,384]{2,0,1:T(8,128)}), f32[48,3,384]{2,0,1:T(8,128)}) %reduce-scatter.35.cloned.1.call-update) | async-done | bytes 221200 | tf_op jit(solution)/shard_map/reduce_scatter | solution.py:349
  1750.7 70.9 %reduce-scatter.33.cloned.1.call-done = f32[48,3,384]{2,0,1:T(8,128)} async-done(((f32[768,3,384]{2,0,1:T(8,128)}), f32[48,3,384]{2,0,1:T(8,128)}) %reduce-scatter.33.cloned.1.call-update) | async-done | bytes 221200 | tf_op jit(solution)/shard_map/reduce_scatter | solution.py:349
  (478 shorter events, 638.0 us)
Async XLA Ops:
  9.0 200.2 %reduce-scatter.17.cloned.1.call-start = ((), (), s32[]{:S(2)}) async-start(), calls=%async_computation.16 | async-start | bytes 3538944 | tf_op jit(solution)/shard_map/reduce_scatter | solution.py:108
  61.8 48.8 %collective-permute-start.2 = (bf16[768,768]{0,1:T(8,128)(2,1)}, bf16[768,768]{0,1:T(8,128)(2,1)}, u32[]{:S(2)}, u32[]{:S(2)}) collective-permute-start(bf16[768,768]{0,1:T(8,128)(2,1)} %bitcast.6), channel_id=1, source_target_pairs={{2,0},{4,2},{6,4},{8,6},{10,8},{12,10},{14,12},{16,14},{18,16},{20... | collective-permute-start | bytes 3538952 | tf_op jit(solution)/shard_map/ppermute | solution.py:30
  63.1 47.5 %collective-permute-start.1 = (bf16[768,768]{0,1:T(8,128)(2,1)}, bf16[768,768]{0,1:T(8,128)(2,1)}, u32[]{:S(2)}, u32[]{:S(2)}) collective-permute-start(bf16[768,768]{0,1:T(8,128)(2,1)} %bitcast.6), channel_id=1, source_target_pairs={{0,2},{2,4},{4,6},{6,8},{8,10},{10,12},{12,14},{14,16},{16,18},{18... | collective-permute-start | bytes 3538952 | tf_op jit(solution)/shard_map/ppermute | solution.py:27
  174.4 79.9 %all-gather.17.cloned.1.call-start = ((), (), s32[]{:S(2)}) async-start(), calls=%async_computation.33 | async-start | bytes 2506752 | tf_op jit(solution)/shard_map/all_gather | solution.py:98
  176.2 121.9 %all-gather.19.cloned.1.call-start = ((), (), s32[]{:S(2)}) async-start(), calls=%async_computation.34 | async-start | bytes 2506752 | tf_op jit(solution)/shard_map/all_gather | solution.py:99
  177.9 159.6 %reduce-scatter.19.cloned.1.call-start = ((), (), s32[]{:S(2)}) async-start(), calls=%async_computation.17 | async-start | bytes 3538944 | tf_op jit(solution)/shard_map/reduce_scatter | solution.py:108
  303.9 76.8 %all-gather.21.cloned.1.call-start = ((), (), s32[]{:S(2)}) async-start(), calls=%async_computation.35 | async-start | bytes 1880064 | tf_op jit(solution)/shard_map/all_gather | solution.py:96
  304.4 237.8 %reduce-scatter.21.cloned.1.call-start = ((), (), s32[]{:S(2)}) async-start(), calls=%async_computation.18 | async-start | bytes 3538944 | tf_op jit(solution)/shard_map/reduce_scatter | solution.py:108
  494.6 92.5 %all-gather.23.cloned.1.call-start = ((), (), s32[]{:S(2)}) async-start(), calls=%async_computation.36 | async-start | bytes 2506752 | tf_op jit(solution)/shard_map/all_gather | solution.py:98
  495.4 135.1 %all-gather.25.cloned.1.call-start = ((), (), s32[]{:S(2)}) async-start(), calls=%async_computation.37 | async-start | bytes 2506752 | tf_op jit(solution)/shard_map/all_gather | solution.py:99
  496.1 179.3 %reduce-scatter.25.cloned.1.call-start = ((), (), s32[]{:S(2)}) async-start(), calls=%async_computation.20 | async-start | bytes 3538944 | tf_op jit(solution)/shard_map/reduce_scatter | solution.py:108
  641.8 70.8 %reduce-scatter.23.cloned.1.call-start = ((), (), s32[]{:S(2)}) async-start(), calls=%async_computation.19 | async-start | bytes 3538944 | tf_op jit(solution)/shard_map/reduce_scatter | solution.py:108
  647.7 227.6 %reduce-scatter.27.cloned.1.call-start = ((), (), s32[]{:S(2)}) async-start(), calls=%async_computation.21 | async-start | bytes 3538944 | tf_op jit(solution)/shard_map/reduce_scatter | solution.py:108
  835.5 108.9 %reduce-scatter.29.cloned.1.call-start = ((), (), s32[]{:S(2)}) async-start(), calls=%async_computation.22 | async-start | bytes 3538944 | tf_op jit(solution)/shard_map/reduce_scatter | solution.py:108
  909.5 214.8 %reduce-scatter.31.cloned.1.call-start = ((), (), s32[]{:S(2)}) async-start(), calls=%async_computation.23 | async-start | bytes 3538944 | tf_op jit(solution)/shard_map/reduce_scatter | solution.py:108
  1067.1 101.0 %reduce-scatter.39.cloned.1.call-start = ((), (), s32[]{:S(2)}) async-start(), calls=%async_computation.27 | async-start | bytes 1253376 | tf_op jit(solution)/shard_map/reduce_scatter | solution.py:350
  1070.2 158.7 %reduce-scatter.37.cloned.1.call-start = ((), (), s32[]{:S(2)}) async-start(), calls=%async_computation.26 | async-start | bytes 1253376 | tf_op jit(solution)/shard_map/reduce_scatter | solution.py:350
  1072.0 235.3 %reduce-scatter.47.cloned.1.call-start = ((), (), s32[]{:S(2)}) async-start(), calls=%async_computation.31 | async-start | bytes 5013504 | tf_op jit(solution)/shard_map/reduce_scatter | solution.py:352
  1078.0 307.9 %reduce-scatter.45.cloned.1.call-start = ((), (), s32[]{:S(2)}) async-start(), calls=%async_computation.30 | async-start | bytes 5013504 | tf_op jit(solution)/shard_map/reduce_scatter | solution.py:352
  1084.4 380.1 %reduce-scatter.43.cloned.1.call-start = ((), (), s32[]{:S(2)}) async-start(), calls=%async_computation.29 | async-start | bytes 5013504 | tf_op jit(solution)/shard_map/reduce_scatter | solution.py:351
  1090.7 452.3 %reduce-scatter.41.cloned.1.call-start = ((), (), s32[]{:S(2)}) async-start(), calls=%async_computation.28 | async-start | bytes 5013504 | tf_op jit(solution)/shard_map/reduce_scatter | solution.py:351
  1096.9 578.7 %all-reduce.3.cloned.1.call-start = ((), (), s32[]{:S(2)}) async-start(), calls=%async_computation.38 | async-start | bytes 147456 | tf_op jit(solution)/shard_map/psum | solution.py:354
  1128.1 622.6 %reduce-scatter.35.cloned.1.call-start = ((), (), s32[]{:S(2)}) async-start(), calls=%async_computation.25 | async-start | bytes 3760128 | tf_op jit(solution)/shard_map/reduce_scatter | solution.py:349
  1133.0 688.6 %reduce-scatter.33.cloned.1.call-start = ((), (), s32[]{:S(2)}) async-start(), calls=%async_computation.24 | async-start | bytes 3760128 | tf_op jit(solution)/shard_map/reduce_scatter | solution.py:349
  (125 other events, 3302.8 us)
Sparse Core Ops, SparseCore 0:
  10.9 43.0 all-gather.14
  174.5 34.7 reduce-scatter.16
  212.1 42.0 all-gather.16
  257.0 41.0 all-gather.18
  304.0 33.5 reduce-scatter.18
  340.3 40.3 all-gather.20
  494.8 47.3 reduce-scatter.20
  545.1 42.0 all-gather.22
  589.4 41.0 all-gather.24
  641.9 33.5 reduce-scatter.24
  677.7 34.7 reduce-scatter.22
  835.7 39.5 reduce-scatter.26
  909.6 34.7 reduce-scatter.28
  1067.2 39.2 reduce-scatter.30
  1110.0 58.0 reduce-scatter.38
  1171.6 57.2 reduce-scatter.36
  1232.6 74.6 reduce-scatter.46
  1311.0 74.7 reduce-scatter.44
  1389.7 74.7 reduce-scatter.42
  1468.2 74.7 reduce-scatter.40
  1550.6 124.9 all-reduce.2
  1679.5 71.1 reduce-scatter.34
  1754.6 66.9 reduce-scatter.32
